TPU v7x, 256 devices: a whole 4x4x8 slice. The times are simulated.
256 devices in a mesh: row: 16 (over x, y_hi, core), col: 16 (over z, y_lo).
Axes of the slice: x: 4, y: 4 (y_hi: 2, y_lo: 2; y = y_hi * 2 + y_lo), z: 8, core: 2. Of those that a mesh axis runs over, the one named last changes fastest.
Arguments:
- positions: float32 [3, 16384], P(None, ('row', 'col')), may hold values from -0.2 to 63.2, as said below
- radii: float32 [16384], P(('row', 'col')), may hold values from 0.1 to 0.28
- basis: float32 [32, 3, 16384], P(None, None, ('row', 'col')), may hold values from -0.0112763724 to 0.0112763724, as said below
- rhs: float32 [3, 16384], P(None, ('row', 'col')), may hold values from -6 to 6
Outputs:
- solution: float32 [3, 16384], P(None, ('row', 'col'))
- residual: float32 [3, 16384], P(None, ('row', 'col'))
Inputs may be any that keep to these rules, and one draw needn't show every extreme that they name: `positions`: every coordinate lies within 0.2 of a whole number and any two centres are 0.6 or more apart, more than the sum of any two radii. `basis`: the 32 vectors are linearly independent.
All inputs are finite; a program needn't handle non-finite values.
Results may differ from a plain program's by a relative error of at most 0.0003.
Values sent between devices are 32-bit elements; how exact they have to be, the bound alone decides.
A program may use at most 64 MiB of HBM per device.

v0:
```python
import math
import jax
import jax.numpy as jnp
from jax import lax
from jax.sharding import PartitionSpec as P

ITERS = 2
far_scale = 1.0 / (8.0 * math.pi)
self_scale = 1.0 / (6.0 * math.pi)
highest = lax.Precision.HIGHEST


def contract(left, right):
    return lax.dot_general(
        left, right, (((1,), (1,)), ((), ())), precision=highest, preferred_element_type=jnp.float32
    )


def block_apply(out_pos, out_rad, out_index, in_pos, in_rad, in_index, fields):
    deltas = [out_pos[axis_id][:, None] - in_pos[axis_id][None, :] for axis_id in range(3)]
    coincide = out_index[:, None] == in_index[None, :]
    dist_sq = deltas[0] * deltas[0] + deltas[1] * deltas[1] + deltas[2] * deltas[2]
    safe_sq = jnp.where(coincide, jnp.ones_like(dist_sq), dist_sq)
    inv_sq = 1.0 / safe_sq
    inv_dist = jnp.sqrt(inv_sq)
    radius_sum = (out_rad * out_rad)[:, None] + (in_rad * in_rad)[None, :]
    scaled = far_scale * inv_dist
    isotropic = scaled * (1.0 + radius_sum * inv_sq / 3.0)
    own_term = jnp.broadcast_to((self_scale / out_rad)[:, None], isotropic.shape)
    isotropic = jnp.where(coincide, own_term, isotropic)
    along = jnp.where(
        coincide, jnp.zeros_like(dist_sq), scaled * (1.0 - radius_sum * inv_sq) * inv_sq
    )
    tensors = {}
    for first in range(3):
        for second in range(first, 3):
            entry = along * deltas[first] * deltas[second]
            if first == second:
                entry = entry + isotropic
            tensors[first, second] = entry
    results = []
    for first in range(3):
        total = None
        for second in range(3):
            term = contract(fields[:, second, :], tensors[min(first, second), max(first, second)])
            total = term if total is None else total + term
        results.append(total)
    return jnp.stack(results, axis=1)


def field_apply(out_pos, out_rad, out_index, in_pos, in_rad, in_index, fields, width):
    count = out_rad.shape[0] // width
    pos_blocks = out_pos.reshape(3, count, width).transpose(1, 0, 2)
    rad_blocks = out_rad.reshape(count, width)
    index_blocks = out_index.reshape(count, width)

    def one_block(packed):
        return block_apply(packed[0], packed[1], packed[2], in_pos, in_rad, in_index, fields)

    stacked = lax.map(one_block, (pos_blocks, rad_blocks, index_blocks))
    return stacked.transpose(1, 2, 0, 3).reshape(fields.shape[0], 3, count * width)


def body(positions, radii, basis, rhs):
    cols_count = lax.axis_size("col")
    row_id = lax.axis_index("row")
    col_id = lax.axis_index("col")
    width = positions.shape[1]
    vectors_count = basis.shape[0]
    target_pos, target_rad = (
        lax.all_gather(positions, "row", axis=1, tiled=True),
        lax.all_gather(radii, "row", axis=0, tiled=True),
    )
    source_pos, source_rad = (
        lax.all_gather(positions, "col", axis=1, tiled=True),
        lax.all_gather(radii, "col", axis=0, tiled=True),
    )
    target_span = target_rad.shape[0]
    source_span = source_rad.shape[0]
    target_order = jnp.arange(target_span, dtype=jnp.int32)
    target_index = (target_order // width * cols_count + col_id) * width + target_order % width
    source_index = row_id * (cols_count * width) + jnp.arange(source_span, dtype=jnp.int32)

    def fold_sources(carry, piece):
        count = piece.shape[2]
        in_pos = lax.slice_in_dim(source_pos, 0, count, axis=1)
        in_rad = lax.slice_in_dim(source_rad, 0, count, axis=0)
        in_index = lax.slice_in_dim(source_index, 0, count, axis=0)
        return carry + field_apply(
            target_pos, target_rad, target_index, in_pos, in_rad, in_index, piece, width
        )

    empty_rows = jnp.zeros((vectors_count, 3, target_span), jnp.float32)
    partial_basis = fold_sources(
        empty_rows, jax.tree.map(lambda a: lax.all_gather(a, "col", axis=2, tiled=True), basis)
    )
    basis_image = lax.psum_scatter(partial_basis, "row", scatter_dimension=2, tiled=True)
    gram_part = jnp.einsum("kcp,lcp->kl", basis, basis_image, precision=highest)
    load_part = jnp.einsum("kcp,cp->k", basis, rhs, precision=highest)
    gram, load = lax.psum((gram_part, load_part), ("row", "col"))
    factor = jnp.linalg.cholesky(gram)

    def coarse_solve(vector):
        return jax.scipy.linalg.cho_solve((factor, True), vector)

    def combine(weights, fields):
        return jnp.einsum("k,kcp->cp", weights, fields, precision=highest)

    def correlation_of(field):
        return jnp.einsum("kcp,cp->k", basis_image, field, precision=highest)

    coarse = coarse_solve(load)
    solution = combine(coarse, basis)
    residual = rhs - combine(coarse, basis_image)

    def residual_stats(field):
        return lax.psum((correlation_of(field), jnp.sum(field * field)), ("row", "col"))

    correlation, norm_now = residual_stats(residual)
    projection = coarse_solve(correlation)
    direction = residual - combine(projection, basis)
    for iteration in range(ITERS):
        empty = jnp.zeros((1, 3, target_span), jnp.float32)
        partial_image = fold_sources(
            empty,
            jax.tree.map(lambda a: lax.all_gather(a, "col", axis=2, tiled=True), direction[None]),
        )
        image = lax.psum_scatter(partial_image, "row", scatter_dimension=2, tiled=True)[0]
        curvature = lax.psum(jnp.sum(direction * image), ("row", "col"))
        step_size = norm_now / curvature
        solution = solution + step_size * direction
        residual = residual - step_size * image
        if iteration + 1 < ITERS:
            correlation, norm_next = residual_stats(residual)
            projection = coarse_solve(correlation)
            direction = residual + norm_next / norm_now * direction - combine(projection, basis)
            norm_now = norm_next
    return (solution, residual)


def solution(mesh):
    return jax.shard_map(
        body,
        mesh=mesh,
        in_specs=(
            P(None, ("row", "col")),
            P(("row", "col")),
            P(None, None, ("row", "col")),
            P(None, ("row", "col")),
        ),
        out_specs=(P(None, ("row", "col")), P(None, ("row", "col"))),
        check_vma=False,
    )
```

profile of v0, /device:TPU:1, one launch (start us, length us, event | category | flops | bytes accessed | tf_op | source)
XLA Modules:
  0.0 1161.8 jit_solution(4575639744863065165)
XLA Ops:
  7.2 26.0 %all-gather.2 = f32[16,64,3]{1,2,0:T(4,128)S(1)} all-gather(f32[1,64,3]{1,2,0:T(4,128)} %bitcast.659), channel_id=1, replica_groups=mesh['row'=16,'col'=16] {'row'}, dimensions={0}, use_global_device_ids=true | all-gather | bytes 13056 | tf_op jit(solution)/shard_map/all_gather | solution.py:71
  33.2 28.7 %all-gather.3 = f32[16,64,3]{1,2,0:T(4,128)S(1)} all-gather(f32[1,64,3]{1,2,0:T(4,128)} %bitcast.660), channel_id=1, replica_groups=mesh['row'=16,'col'=16] {'col'}, dimensions={0}, use_global_device_ids=true | all-gather | bytes 13056 | tf_op jit(solution)/shard_map/all_gather | solution.py:75
  61.8 1.3 dynamic-slice
  63.8 0.9 dynamic-update-slice.3
  64.6 39.9 %all-reduce = f32[1024]{0:T(1024)S(1)} all-reduce(f32[1024]{0:T(1024)S(1)} %dynamic-update-slice.3), channel_id=1, replica_groups=mesh['row'=16,'col'=16] {'row'}, use_global_device_ids=true, to_apply=%add | all-reduce | flops 1024 | bytes 8192
  104.6 1.3 dynamic-slice.1
  106.5 0.9 dynamic-update-slice.4
  107.4 23.7 %all-reduce.1 = f32[1024]{0:T(1024)S(1)} all-reduce(f32[1024]{0:T(1024)S(1)} %dynamic-update-slice.4), channel_id=1, replica_groups=mesh['row'=16,'col'=16] {'col'}, use_global_device_ids=true, to_apply=%add.1 | all-reduce | flops 1024 | bytes 8192
  131.4 0.9 copy.39
  132.3 49.4 %all_gather.25 = f32[32,3,1024]{0,1,2:T(4,128)S(1)} all-gather(f32[32,3,64]{0,1,2:T(4,128)S(1)} %copy.39), channel_id=1, replica_groups=mesh['row'=16,'col'=16] {'col'}, dimensions={2}, use_global_device_ids=true | all-gather | bytes 417792 | tf_op jit(solution)/shard_map/all_gather | solution.py:95
  181.7 0.8 copy.41
  182.6 103.6 %while.39 = (s32[]{:T(128)}, f32[16,32,3,64]{3,1,2,0:T(8,128)S(1)}, s32[16,64]{1,0:T(8,128)S(1)}, f32[16,3,64]{2,1,0:T(4,128)S(1)}, f32[3,1024]{1,0:T(4,128)S(1)...) while((s32[]{:T(128)}, f32[16,32,3,64]{3,1,2,0:T(8,128)S(1)}, ...), condition=%wide.region_1.2_spmd.clone, body=%wide.region_0.1_spmd.clone.sunk | while | flops 239297664 | bytes 2417017 | solution.py:60
  183.0 0.7 fusion.370
  185.6 0.7 convolution_add_fusion.10
  189.4 0.7 fusion.370
  192.1 0.7 convolution_add_fusion.10
  195.9 0.7 fusion.370
  198.6 0.7 convolution_add_fusion.10
  202.4 0.7 fusion.370
  205.1 0.7 convolution_add_fusion.10
  208.9 0.7 fusion.370
  211.6 0.7 convolution_add_fusion.10
  215.4 0.7 fusion.370
  218.0 0.7 convolution_add_fusion.10
  221.8 0.7 fusion.370
  224.5 0.7 convolution_add_fusion.10
  228.3 0.7 fusion.370
  231.0 0.7 convolution_add_fusion.10
  234.8 0.7 fusion.370
  237.5 0.7 convolution_add_fusion.10
  241.3 0.7 fusion.370
  243.9 0.7 convolution_add_fusion.10
  247.7 0.7 fusion.370
  250.4 0.7 convolution_add_fusion.10
  254.2 0.7 fusion.370
  256.9 0.7 convolution_add_fusion.10
  260.7 0.7 fusion.370
  267.2 0.7 fusion.370
  273.7 0.7 fusion.370
  280.1 0.7 fusion.370
  282.8 0.7 convolution_add_fusion.10
  286.2 0.9 copy.64
  287.2 1.5 reshape.352
  288.9 75.8 %reduce-scatter.10.cloned.1.call-done = f32[64,96]{1,0:T(8,128)} async-done(((f32[1024,96]{1,0:T(8,128)}), f32[64,96]{1,0:T(8,128)}) %reduce-scatter.10.cloned.1.call-update) | async-done | bytes 24592
  364.8 0.9 reshape.353
  366.0 77.7 %all-reduce.4 = (f32[32,32]{0,1:T(8,128)S(1)}, f32[32]{0:T(128)S(1)}) all-reduce(f32[32,32]{0,1:T(8,128)S(1)} %convolution_bitcast_fusion.18, f32[32]{0:T(128)S(1)} %convolution_bitcast_fusion.27), channel_id=1, replica_groups=mesh['row'=16,'col'=16] {'row','col'}, use_global_device_ids=true, to_apply=%region_3.4 | all-reduce | flops 1056 | bytes 8448 | tf_op jit(solution)/shard_map/psum | solution.py:100
  443.7 2.9 cholesky.18
  447.9 2.4 custom-call.10
  451.6 73.1 %psum.59 = f32[32]{0:T(128)S(1)} all-reduce(f32[32]{0:T(128)S(1)} %convolution_bitcast_fusion.26), channel_id=1, replica_groups=mesh['row'=16,'col'=16] {'row','col'}, use_global_device_ids=true, to_apply=%region_9.11 | all-reduce | flops 32 | bytes 256 | tf_op jit(solution)/shard_map/psum | solution.py:117
  525.1 24.3 %all-gather.4 = f32[16,64,3]{1,2,0:T(4,128)S(1)} all-gather(f32[1,64,3]{1,2,0:T(4,128)S(1)} %bitcast.652), channel_id=2, replica_groups=mesh['row'=16,'col'=16] {'col'}, dimensions={0}, use_global_device_ids=true | all-gather | bytes 13056 | tf_op jit(solution)/shard_map/all_gather | solution.py:126
  549.6 95.1 %while.40 = (s32[]{:T(128)}, f32[16,1,3,64]{3,2,1,0:T(4,128)S(1)}, s32[16,64]{1,0:T(8,128)S(1)}, f32[16,3,64]{2,1,0:T(4,128)S(1)}, f32[3,1024]{1,0:T(4,128)S(1)}...) while((s32[]{:T(128)}, f32[16,1,3,64]{3,2,1,0:T(4,128)S(1)}, ...), condition=%wide.region_11.13_spmd.clone, body=%wide.region_10.12_spmd.clone.sunk | while | flops 19859328 | bytes 287865 | solution.py:60
  644.7 0.9 copy.60
  645.6 1.9 bitcast_reduce_fusion
  647.7 74.9 %reduce-scatter.12.cloned.1.call-done = f32[64,3]{1,0:T(8,128)} async-done(((f32[1024,3]{1,0:T(8,128)}), f32[64,3]{1,0:T(8,128)}) %reduce-scatter.12.cloned.1.call-update) | async-done | bytes 784
  722.5 0.9 reshape_bitcast_fusion
  723.5 0.7 fusion.251
  724.2 77.5 %all-reduce.3 = (f32[]{:T(128)}, f32[]{:T(128)}) all-reduce(f32[]{:T(128)} %get-tuple-element.527, f32[]{:T(128)} %fusion.251), channel_id=1, replica_groups=mesh['row'=16,'col'=16] {'row','col'}, use_global_device_ids=true, to_apply=%region_8.10 | all-reduce | flops 2 | bytes 16 | tf_op jit(solution)/shard_map/psum | solution.py:117
  804.0 73.6 %all-reduce.2 = (f32[32]{0:T(128)S(1)}, f32[]{:T(128)}) all-reduce(f32[32]{0:T(128)S(1)} %convolution_bitcast_fusion.25, f32[]{:T(128)} %get-tuple-element.525), channel_id=1, replica_groups=mesh['row'=16,'col'=16] {'row','col'}, use_global_device_ids=true, to_apply=%region_17.19 | all-reduce | flops 33 | bytes 264 | tf_op jit(solution)/shard_map/psum | solution.py:117
  879.3 23.9 %all-gather.5 = f32[16,64,3]{1,2,0:T(4,128)S(1)} all-gather(f32[1,64,3]{1,2,0:T(4,128)S(1)} %bitcast.654), channel_id=3, replica_groups=mesh['row'=16,'col'=16] {'col'}, dimensions={0}, use_global_device_ids=true | all-gather | bytes 13056 | tf_op jit(solution)/shard_map/all_gather | solution.py:126
  903.2 95.1 %while.41 = (s32[]{:T(128)}, f32[16,1,3,64]{3,2,1,0:T(4,128)S(1)}, s32[16,64]{1,0:T(8,128)S(1)}, f32[16,3,64]{2,1,0:T(4,128)S(1)}, f32[3,1024]{1,0:T(4,128)S(1)}...) while((s32[]{:T(128)}, f32[16,1,3,64]{3,2,1,0:T(4,128)S(1)}, ...), condition=%wide.region_19.21_spmd.clone, body=%wide.region_18.20_spmd.clone.sunk | while | flops 19859328 | bytes 287865 | solution.py:60
  998.3 1.0 copy.65
  999.4 74.9 %reduce-scatter.14.cloned.1.call-done = f32[64,3]{1,0:T(8,128)} async-done(((f32[1024,3]{1,0:T(8,128)}), f32[64,3]{1,0:T(8,128)}) %reduce-scatter.14.cloned.1.call-update) | async-done | bytes 784
  1074.3 0.8 copy.63
  1075.9 77.5 %psum.63 = f32[]{:T(128)} all-reduce(f32[]{:T(128)} %fusion.253), channel_id=1, replica_groups=mesh['row'=16,'col'=16] {'row','col'}, use_global_device_ids=true, to_apply=%region_22.24 | all-reduce | flops 1 | bytes 8 | tf_op jit(solution)/shard_map/psum | solution.py:129
  (812 shorter events, 274.4 us)
Async XLA Ops:
  7.2 357.6 %reduce-scatter.10.cloned.1.call-start = ((), (), s32[]{:S(2)}) async-start(), calls=%async_computation.3 | async-start | bytes 557056
  287.2 1.6 copy-start
  287.2 1.6 copy-start.1
  288.7 433.8 %reduce-scatter.12.cloned.1.call-start = ((), (), s32[]{:S(2)}) async-start(), calls=%async_computation.4 | async-start | bytes 557056
  647.6 426.7 %reduce-scatter.14.cloned.1.call-start = ((), (), s32[]{:S(2)}) async-start(), calls=%async_computation.5 | async-start | bytes 557056
Sparse Core Ops, SparseCore 0:
  288.9 75.8 reduce-scatter.9
  647.7 74.7 reduce-scatter.11
  999.5 74.7 reduce-scatter.13
where the time goes:
time: 1160 us
  blocking collectives  595 us (51%)
  matrix products  281 us (24%)
  waiting for transfers between devices  226 us (19%)
  local copies, waits for them, and re-layouts  21.8 us (2%)
  between operations  19.2 us (2%)
  other arithmetic  13.2 us (1%)
    dot_general x432, matrix products, contract(): lax.dot_general(left, right, (((1,), (1,)), ((), ())), precision=highest,...  278 us
    unnamed x6, waiting for transfers between devices  226 us
    psum x3, blocking collectives, residual_stats(): lax.psum((correlation_of(field), jnp.sum(field * field)), ('row', 'col'))  224 us
    all_gather x3, blocking collectives, body(): lax.all_gather(a, 'col', axis=2, tiled=True)  97.6 us
    psum x1, blocking collectives, body(): gram, load = lax.psum((gram_part, load_part), ('row', 'col'))  77.7 us
    psum x1, blocking collectives, body(): curvature = lax.psum(jnp.sum(direction * image), ('row', 'col'))  77.5 us
    unnamed x2, blocking collectives  63.6 us
    all_gather x1, blocking collectives, body(): lax.all_gather(positions, 'col', axis=1, tiled=True)  28.7 us
  transfers between devices with their start and end apart: 3, of which 3 were waited for; matrix products, arithmetic and copies ran while one was open for 0% of the time, Pallas kernels for 0%

commit v1 on v0

--- a/solution.py
+++ b/solution.py
@@ -8,6 +8,12 @@
 far_scale = 1.0 / (8.0 * math.pi)
 self_scale = 1.0 / (6.0 * math.pi)
 highest = lax.Precision.HIGHEST
+
+
+def weights_answer(piece_in, comm_axis, lane_axis):
+    for at in (comm_axis, lane_axis):
+        piece_in = jax.lax.psum(piece_in, at)
+    return piece_in
 
 
 def contract(left, right):
@@ -114,7 +120,7 @@
     residual = rhs - combine(coarse, basis_image)
 
     def residual_stats(field):
-        return lax.psum((correlation_of(field), jnp.sum(field * field)), ("row", "col"))
+        return weights_answer((correlation_of(field), jnp.sum(field * field)), "row", "col")
 
     correlation, norm_now = residual_stats(residual)
     projection = coarse_solve(correlation)

time: 1160 us -> 1150 us (level)
  blocking collectives: 595 us -> 566 us
  waiting for transfers between devices: 226 us -> 240 us
    psum x3 -> x4, blocking collectives: 224 us -> 118 us  [weights_answer(): piece_in = jax.lax.psum(piece_in, at)]
    psum x1 -> x2, blocking collectives: 77.5 us -> 155 us  [body(): curvature = lax.psum(jnp.sum(direction * image), ('row', 'col'))]
    unnamed x6, waiting for transfers between devices: 226 us -> 240 us
where the time goes in v1:
time: 1150 us
  blocking collectives  566 us (49%)
  matrix products  281 us (24%)
  waiting for transfers between devices  240 us (21%)
  local copies, waits for them, and re-layouts  21.8 us (2%)
  between operations  19.2 us (2%)
  other arithmetic  13.1 us (1%)
    dot_general x432, matrix products, contract(): lax.dot_general(left, right, (((1,), (1,)), ((), ())), precision=highest,...  279 us
    unnamed x6, waiting for transfers between devices  240 us
    psum x2, blocking collectives, body(): curvature = lax.psum(jnp.sum(direction * image), ('row', 'col'))  155 us
    psum x4, blocking collectives, weights_answer(): piece_in = jax.lax.psum(piece_in, at)  118 us
    all_gather x3, blocking collectives, body(): lax.all_gather(a, 'col', axis=2, tiled=True)  97.4 us
    psum x1, blocking collectives, body(): gram, load = lax.psum((gram_part, load_part), ('row', 'col'))  77.7 us
    unnamed x2, blocking collectives  63.6 us
    all_gather x1, blocking collectives, body(): lax.all_gather(positions, 'col', axis=1, tiled=True)  28.7 us
  transfers between devices with their start and end apart: 3, of which 3 were waited for; matrix products, arithmetic and copies ran while one was open for 0% of the time, Pallas kernels for 0%

profile of v1, /device:TPU:1, one launch (start us, length us, event | category | flops | bytes accessed | tf_op | source)
XLA Modules:
  0.0 1147.0 jit_solution(7517966851679531718)
XLA Ops:
  7.2 26.0 %all-gather.2 = f32[16,64,3]{1,2,0:T(4,128)S(1)} all-gather(f32[1,64,3]{1,2,0:T(4,128)} %bitcast.659), channel_id=1, replica_groups=mesh['row'=16,'col'=16] {'row'}, dimensions={0}, use_global_device_ids=true | all-gather | bytes 13056 | tf_op jit(solution)/shard_map/all_gather | solution.py:77
  33.2 28.7 %all-gather.3 = f32[16,64,3]{1,2,0:T(4,128)S(1)} all-gather(f32[1,64,3]{1,2,0:T(4,128)} %bitcast.660), channel_id=1, replica_groups=mesh['row'=16,'col'=16] {'col'}, dimensions={0}, use_global_device_ids=true | all-gather | bytes 13056 | tf_op jit(solution)/shard_map/all_gather | solution.py:81
  61.8 1.3 dynamic-slice
  63.8 0.9 dynamic-update-slice.3
  64.6 39.9 %all-reduce = f32[1024]{0:T(1024)S(1)} all-reduce(f32[1024]{0:T(1024)S(1)} %dynamic-update-slice.3), channel_id=1, replica_groups=mesh['row'=16,'col'=16] {'row'}, use_global_device_ids=true, to_apply=%add | all-reduce | flops 1024 | bytes 8192
  104.6 1.3 dynamic-slice.1
  106.5 0.9 dynamic-update-slice.4
  107.4 23.7 %all-reduce.1 = f32[1024]{0:T(1024)S(1)} all-reduce(f32[1024]{0:T(1024)S(1)} %dynamic-update-slice.4), channel_id=1, replica_groups=mesh['row'=16,'col'=16] {'col'}, use_global_device_ids=true, to_apply=%add.1 | all-reduce | flops 1024 | bytes 8192
  131.4 0.9 copy.39
  132.3 49.4 %all_gather.25 = f32[32,3,1024]{0,1,2:T(4,128)S(1)} all-gather(f32[32,3,64]{0,1,2:T(4,128)S(1)} %copy.39), channel_id=1, replica_groups=mesh['row'=16,'col'=16] {'col'}, dimensions={2}, use_global_device_ids=true | all-gather | bytes 417792 | tf_op jit(solution)/shard_map/all_gather | solution.py:101
  181.7 0.8 copy.41
  182.6 103.7 %while.39 = (s32[]{:T(128)}, f32[16,32,3,64]{3,1,2,0:T(8,128)S(1)}, s32[16,64]{1,0:T(8,128)S(1)}, f32[16,3,64]{2,1,0:T(4,128)S(1)}, f32[3,1024]{1,0:T(4,128)S(1)...) while((s32[]{:T(128)}, f32[16,32,3,64]{3,1,2,0:T(8,128)S(1)}, ...), condition=%wide.region_1.2_spmd.clone, body=%wide.region_0.1_spmd.clone.sunk | while | flops 239297664 | bytes 2417017 | solution.py:66
  183.0 0.7 fusion.370
  185.6 0.7 convolution_add_fusion.10
  189.4 0.7 fusion.370
  192.1 0.7 convolution_add_fusion.10
  195.9 0.7 fusion.370
  198.6 0.7 convolution_add_fusion.10
  202.4 0.7 fusion.370
  205.1 0.7 convolution_add_fusion.10
  208.9 0.7 fusion.370
  215.4 0.7 fusion.370
  218.1 0.7 convolution_add_fusion.10
  221.9 0.7 fusion.370
  228.3 0.7 fusion.370
  231.0 0.7 convolution_add_fusion.10
  234.8 0.7 fusion.370
  237.5 0.7 convolution_add_fusion.10
  241.3 0.7 fusion.370
  244.0 0.7 convolution_add_fusion.10
  247.8 0.7 fusion.370
  254.3 0.7 fusion.370
  256.9 0.7 convolution_add_fusion.10
  260.7 0.7 fusion.370
  267.2 0.7 fusion.370
  269.9 0.7 convolution_add_fusion.10
  273.7 0.7 fusion.370
  276.4 0.7 convolution_add_fusion.10
  280.2 0.7 fusion.370
  286.3 0.9 copy.64
  287.2 1.5 reshape.352
  289.0 75.8 %reduce-scatter.10.cloned.1.call-done = f32[64,96]{1,0:T(8,128)} async-done(((f32[1024,96]{1,0:T(8,128)}), f32[64,96]{1,0:T(8,128)}) %reduce-scatter.10.cloned.1.call-update) | async-done | bytes 24592
  364.9 0.9 reshape.353
  366.0 77.7 %all-reduce.2 = (f32[32,32]{0,1:T(8,128)S(1)}, f32[32]{0:T(128)S(1)}) all-reduce(f32[32,32]{0,1:T(8,128)S(1)} %convolution_bitcast_fusion.18, f32[32]{0:T(128)S(1)} %convolution_bitcast_fusion.27), channel_id=1, replica_groups=mesh['row'=16,'col'=16] {'row','col'}, use_global_device_ids=true, to_apply=%region_3.4 | all-reduce | flops 1056 | bytes 8448 | tf_op jit(solution)/shard_map/psum | solution.py:106
  443.7 2.9 cholesky.18
  448.0 2.4 custom-call.10
  451.7 34.1 %all-reduce.6 = (f32[32]{0:T(128)S(1)}, f32[]{:T(128)}) all-reduce(f32[32]{0:T(128)S(1)} %convolution_bitcast_fusion.26, f32[]{:T(128)} %get-tuple-element.531), channel_id=1, replica_groups=mesh['row'=16,'col'=16] {'row'}, use_global_device_ids=true, to_apply=%region_10.12 | all-reduce | flops 33 | bytes 264 | tf_op jit(solution)/shard_map/psum | solution.py:15
  485.8 24.9 %all-reduce.4 = (f32[32]{0:T(128)S(1)}, f32[]{:T(128)}) all-reduce(f32[32]{0:T(128)S(1)} %get-tuple-element.527, f32[]{:T(128)} %get-tuple-element.528), channel_id=1, replica_groups=mesh['row'=16,'col'=16] {'col'}, use_global_device_ids=true, to_apply=%region_11.13 | all-reduce | flops 33 | bytes 264 | tf_op jit(solution)/shard_map/psum | solution.py:15
  511.1 24.0 %all-gather.4 = f32[16,64,3]{1,2,0:T(4,128)S(1)} all-gather(f32[1,64,3]{1,2,0:T(4,128)S(1)} %bitcast.652), channel_id=2, replica_groups=mesh['row'=16,'col'=16] {'col'}, dimensions={0}, use_global_device_ids=true | all-gather | bytes 13056 | tf_op jit(solution)/shard_map/all_gather | solution.py:132
  535.2 95.2 %while.40 = (s32[]{:T(128)}, f32[16,1,3,64]{3,2,1,0:T(4,128)S(1)}, s32[16,64]{1,0:T(8,128)S(1)}, f32[16,3,64]{2,1,0:T(4,128)S(1)}, f32[3,1024]{1,0:T(4,128)S(1)}...) while((s32[]{:T(128)}, f32[16,1,3,64]{3,2,1,0:T(4,128)S(1)}, ...), condition=%wide.region_13.15_spmd.clone, body=%wide.region_12.14_spmd.clone.sunk | while | flops 19859328 | bytes 287865 | solution.py:66
  630.5 0.9 copy.60
  631.4 1.9 bitcast_reduce_fusion
  633.4 82.0 %reduce-scatter.12.cloned.1.call-done = f32[64,3]{1,0:T(8,128)} async-done(((f32[1024,3]{1,0:T(8,128)}), f32[64,3]{1,0:T(8,128)}) %reduce-scatter.12.cloned.1.call-update) | async-done | bytes 784
  715.4 0.9 reshape_bitcast_fusion
  716.4 0.7 fusion.251
  717.1 77.4 %psum.90 = f32[]{:T(128)} all-reduce(f32[]{:T(128)} %fusion.251), channel_id=1, replica_groups=mesh['row'=16,'col'=16] {'row','col'}, use_global_device_ids=true, to_apply=%region_16.18 | all-reduce | flops 1 | bytes 8 | tf_op jit(solution)/shard_map/psum | solution.py:135
  796.6 34.1 %all-reduce.5 = (f32[32]{0:T(128)S(1)}, f32[]{:T(128)}) all-reduce(f32[32]{0:T(128)S(1)} %convolution_bitcast_fusion.25, f32[]{:T(128)} %get-tuple-element.529), channel_id=1, replica_groups=mesh['row'=16,'col'=16] {'row'}, use_global_device_ids=true, to_apply=%region_20.22 | all-reduce | flops 33 | bytes 264 | tf_op jit(solution)/shard_map/psum | solution.py:15
  830.7 25.0 %all-reduce.3 = (f32[32]{0:T(128)S(1)}, f32[]{:T(128)}) all-reduce(f32[32]{0:T(128)S(1)} %get-tuple-element.525, f32[]{:T(128)} %get-tuple-element.526), channel_id=1, replica_groups=mesh['row'=16,'col'=16] {'col'}, use_global_device_ids=true, to_apply=%region_21.23 | all-reduce | flops 33 | bytes 264 | tf_op jit(solution)/shard_map/psum | solution.py:15
  857.4 24.0 %all-gather.5 = f32[16,64,3]{1,2,0:T(4,128)S(1)} all-gather(f32[1,64,3]{1,2,0:T(4,128)S(1)} %bitcast.654), channel_id=3, replica_groups=mesh['row'=16,'col'=16] {'col'}, dimensions={0}, use_global_device_ids=true | all-gather | bytes 13056 | tf_op jit(solution)/shard_map/all_gather | solution.py:132
  881.5 95.2 %while.41 = (s32[]{:T(128)}, f32[16,1,3,64]{3,2,1,0:T(4,128)S(1)}, s32[16,64]{1,0:T(8,128)S(1)}, f32[16,3,64]{2,1,0:T(4,128)S(1)}, f32[3,1024]{1,0:T(4,128)S(1)}...) while((s32[]{:T(128)}, f32[16,1,3,64]{3,2,1,0:T(4,128)S(1)}, ...), condition=%wide.region_23.25_spmd.clone, body=%wide.region_22.24_spmd.clone.sunk | while | flops 19859328 | bytes 287865 | solution.py:66
  976.6 1.0 copy.65
  977.7 81.8 %reduce-scatter.14.cloned.1.call-done = f32[64,3]{1,0:T(8,128)} async-done(((f32[1024,3]{1,0:T(8,128)}), f32[64,3]{1,0:T(8,128)}) %reduce-scatter.14.cloned.1.call-update) | async-done | bytes 784
  1059.5 0.8 copy.63
  1061.1 77.5 %psum.95 = f32[]{:T(128)} all-reduce(f32[]{:T(128)} %fusion.253), channel_id=1, replica_groups=mesh['row'=16,'col'=16] {'row','col'}, use_global_device_ids=true, to_apply=%region_26.28 | all-reduce | flops 1 | bytes 8 | tf_op jit(solution)/shard_map/psum | solution.py:135
  (814 shorter events, 275.9 us)
Async XLA Ops:
  7.2 357.7 %reduce-scatter.10.cloned.1.call-start = ((), (), s32[]{:S(2)}) async-start(), calls=%async_computation.3 | async-start | bytes 557056
  287.2 1.6 copy-start
  287.2 1.6 copy-start.1
  288.8 426.6 %reduce-scatter.12.cloned.1.call-start = ((), (), s32[]{:S(2)}) async-start(), calls=%async_computation.4 | async-start | bytes 557056
  633.3 426.2 %reduce-scatter.14.cloned.1.call-start = ((), (), s32[]{:S(2)}) async-start(), calls=%async_computation.5 | async-start | bytes 557056
Sparse Core Ops, SparseCore 0:
  288.9 75.8 reduce-scatter.9
  633.4 81.8 reduce-scatter.11
  977.8 81.6 reduce-scatter.13
